TPU v7x, 256 devices: a whole 4x4x8 slice. The times are simulated.
256 devices in a mesh: row: 32 (over x, y, core), col: 8 (over z).
Axes of the slice: x: 4, y: 4, z: 8, core: 2. Of those that a mesh axis runs over, the one named last changes fastest.
Arguments:
- inputs: bfloat16 [16384, 1792], P(('row', 'col')), may hold values from -6 to 6
- attention_norm_gain: float32 [1792], replicated, may hold values from 0.5 to 1.5
- query_key_value_weight: bfloat16 [1792, 3, 1792], P('row', None, 'col'), may hold values from -0.125 to 0.125
- filter_taps: float32 [3, 2, 1792], P(None, None, 'col'), may hold values from -3 to 3
- output_projection: bfloat16 [1792, 1792], P('col', 'row'), may hold values from -0.125 to 0.125
- window_key_value: bfloat16 [256, 2, 16, 7168], P('row', None, 'col'), may hold values from -300 to 300
- cache_valid_length: int32 [256], P('row'), may hold values from 0 to 64
- lengths: int32 [32, 8], P('row'), may hold values from 1 to 128, 512 in all within a row
- token_adapter_index: int32 [16384, 1], P('row'), may hold values from 0 to 63; in each aligned block of 64 rows (0 to 63, 64 to 127, ...) at most 2 rows name the same one
- adapter_down_map: bfloat16 [64, 1792, 16], P('row'), may hold values from -0.125 to 0.125
- adapter_up_map: bfloat16 [64, 16, 1792], P('row'), may hold values from -1.5 to 1.5
- feed_forward_gain: float32 [1792], replicated, may hold values from 0.5 to 1.5
- gate_projection: bfloat16 [1792, 4096], P('row', 'col'), may hold values from -0.125 to 0.125
- up_projection: bfloat16 [1792, 4096], P('row', 'col'), may hold values from -0.125 to 0.125
- down_projection: bfloat16 [4096, 1792], P('col', 'row'), may hold values from -0.09375 to 0.09375
Outputs:
- layer_out: bfloat16 [16384, 1792], P(('row', 'col'))
Inputs may be any that keep to these rules, and one draw needn't show every extreme that they name: Each row of lengths sums to 512, and its largest entry is exactly 128. `cache_valid_length`: A request with 0 is a new prompt without cached positions. `token_adapter_index`: in each aligned block of 64 tokens no adapter serves more than 2 tokens, and some adapter serves exactly 2.
All inputs are finite; a program needn't handle non-finite values.
Results may differ from a plain program's by a relative error of at most 0.019.
Values may be sent and summed in bfloat16 or wider, within the bound.
A program may use at most 64 MiB of HBM per device.

v0:
```python
import jax
import jax.numpy as jnp
from jax import lax
from jax.sharding import PartitionSpec as P

HD = 112


epsilon = 1e-05


def rms_scaled(values, gain_row):
    mean_square = jnp.mean(values * values, axis=-1, keepdims=True)
    return values * lax.rsqrt(mean_square + epsilon) * gain_row


def layout(lengths_row, tok_count):
    finish = jnp.cumsum(lengths_row)
    begins = finish - lengths_row
    places = jnp.arange(tok_count, dtype=jnp.int32)
    segment = jnp.sum((places[:, None] >= finish[None, :]).astype(jnp.int32), axis=1)
    member = segment[:, None] == jnp.arange(lengths_row.shape[0], dtype=jnp.int32)[None, :]
    inside = places - jnp.sum(jnp.where(member, begins[None, :], 0), axis=1)
    return (segment, inside)


def shifted(values, offset, inside):
    moved_rows = jnp.pad(values[: values.shape[0] - offset], ((offset, 0), (0, 0)))
    return jnp.where((inside >= offset)[:, None], moved_rows, jnp.zeros_like(moved_rows))


def convolve(values, taps, inside):
    running = jnp.zeros_like(values)
    for offset in range(taps.shape[0]):
        running = running + taps[offset][None, :] * shifted(values, offset, inside)
    return running


def make_qkv(qkv_mixed, filter_taps, inside):
    queries = qkv_mixed[:, 0].astype(jnp.bfloat16)
    keys_used = convolve(qkv_mixed[:, 1], filter_taps[:, 0], inside).astype(jnp.bfloat16)
    raw_values = qkv_mixed[:, 2]
    gates = jax.nn.sigmoid(convolve(raw_values, filter_taps[:, 1], inside))
    values_used = (raw_values * gates).astype(jnp.bfloat16)
    return (queries, keys_used, values_used)


def split_cache(window_key_value, head_size):
    requests_here, head_count = (window_key_value.shape[0], window_key_value.shape[2])
    window = window_key_value.shape[3] // head_size
    split_kv = window_key_value.reshape(requests_here, 2, head_count, window, head_size)
    cached_key_rows = jnp.transpose(split_kv[:, 0], (0, 2, 1, 3)).reshape(
        requests_here * window, head_count, head_size
    )
    cached_value_rows = jnp.transpose(split_kv[:, 1], (0, 2, 1, 3)).reshape(
        requests_here * window, head_count, head_size
    )
    return (cached_key_rows, cached_value_rows, window)


def attend(
    queries,
    keys_used,
    values_used,
    window_key_value,
    segment,
    inside,
    cache_valid_length,
    head_size,
):
    tok_count = queries.shape[0]
    head_count = queries.shape[1] // head_size
    requests_here = window_key_value.shape[0]
    cached_key_rows, cached_value_rows, window = split_cache(window_key_value, head_size)
    query_per_head = queries.reshape(tok_count, head_count, head_size)
    key_h = keys_used.reshape(tok_count, head_count, head_size)
    value_per_head = values_used.reshape(tok_count, head_count, head_size)
    attention_score_scale = head_size ** (-0.5)
    places = jnp.arange(tok_count, dtype=jnp.int32)
    local_mask = (
        (segment[:, None] == segment[None, :])
        & (places[None, :] <= places[:, None])
        & (places[None, :] > places[:, None] - window)
    )
    slot_ids = jnp.arange(requests_here * window, dtype=jnp.int32)
    owner_req = slot_ids // window
    within = slot_ids % window
    slot_ages = jnp.repeat(cache_valid_length, window)
    cache_mask = (
        (segment[:, None] == owner_req[None, :])
        & (within[None, :] >= window - slot_ages[None, :])
        & (within[None, :] > inside[:, None])
    )
    local_scores = (
        jnp.einsum("thd,jhd->htj", query_per_head, key_h, preferred_element_type=jnp.float32)
        * attention_score_scale
    )
    cached_score_rows = (
        jnp.einsum(
            "sek,yek->esy", query_per_head, cached_key_rows, preferred_element_type=jnp.float32
        )
        * attention_score_scale
    )
    local_scores = jnp.where(local_mask[None], local_scores, -jnp.inf)
    cached_score_rows = jnp.where(cache_mask[None], cached_score_rows, -jnp.inf)
    row_max = jnp.maximum(
        jnp.max(local_scores, axis=-1, keepdims=True),
        jnp.max(cached_score_rows, axis=-1, keepdims=True),
    )
    local_exp = jnp.exp(local_scores - row_max)
    cache_exp = jnp.exp(cached_score_rows - row_max)
    denominator = jnp.sum(local_exp, axis=-1, keepdims=True) + jnp.sum(
        cache_exp, axis=-1, keepdims=True
    )
    window_attention_weight = (local_exp / denominator).astype(jnp.bfloat16)
    cached_attention_weight = (cache_exp / denominator).astype(jnp.bfloat16)
    joined_output = jnp.einsum(
        "zkc,czu->kzu", window_attention_weight, value_per_head, preferred_element_type=jnp.float32
    )
    joined_output = joined_output + jnp.einsum(
        "lar,rlx->alx",
        cached_attention_weight,
        cached_value_rows,
        preferred_element_type=jnp.float32,
    )
    return joined_output.reshape(tok_count, head_count * head_size).astype(jnp.bfloat16)


def on_device(
    inputs,
    attention_norm_gain,
    query_key_value_weight,
    filter_taps,
    output_projection,
    window_key_value,
    cache_valid_length,
    lengths,
    token_adapter_index,
    adapter_down_map,
    adapter_up_map,
    feed_forward_gain,
    gate_projection,
    up_projection,
    down_projection,
):
    own_count = inputs.shape[0]
    column = lax.axis_index("col")
    row_count = lax.axis_size("row")
    gathered = lax.all_gather(inputs, "col", axis=0, tiled=True)
    tok_count = gathered.shape[0]
    normalized_input = rms_scaled(gathered.astype(jnp.float32), attention_norm_gain).astype(
        jnp.bfloat16
    )
    qkv_mixed = jnp.einsum(
        "td,dka->tka",
        normalized_input,
        lax.all_gather(query_key_value_weight, "row", axis=0, tiled=True),
        preferred_element_type=jnp.float32,
    )
    segment, inside = layout(lengths[0], tok_count)
    queries, keys_used, values_used = make_qkv(qkv_mixed, filter_taps, inside)
    attended = attend(
        queries, keys_used, values_used, window_key_value, segment, inside, cache_valid_length, HD
    )
    kept_count = adapter_down_map.shape[0]
    every_adapter = kept_count * row_count
    capacity = max(2, 2 * own_count // every_adapter)
    first_row = column * own_count
    own_rows = lax.dynamic_slice_in_dim(normalized_input, first_row, own_count, 0)
    own_ids = lax.dynamic_slice_in_dim(token_adapter_index[:, 0], first_row, own_count, 0)
    member = (own_ids[:, None] == jnp.arange(every_adapter, dtype=jnp.int32)[None, :]).astype(
        jnp.int32
    )
    before = jnp.cumsum(member, axis=0) - member
    slot_rank = jnp.sum(before * member, axis=1)
    target = own_ids * capacity + slot_rank
    placer = (
        target[None, :] == jnp.arange(every_adapter * capacity, dtype=jnp.int32)[:, None]
    ).astype(jnp.bfloat16)
    outgoing = jnp.dot(placer, own_rows, preferred_element_type=jnp.float32).astype(jnp.bfloat16)
    outgoing = outgoing.reshape(row_count, kept_count, capacity, normalized_input.shape[1])
    reduced_rank_input = jnp.einsum(
        "sakd,adr->sakr",
        lax.all_to_all(outgoing, "row", split_axis=0, concat_axis=0, tiled=True),
        adapter_down_map,
        preferred_element_type=jnp.float32,
    ).astype(jnp.bfloat16)
    answered = jnp.einsum(
        "zjbf,jfm->zjbm", reduced_rank_input, adapter_up_map, preferred_element_type=jnp.float32
    ).astype(jnp.bfloat16)
    returned = lax.all_to_all(answered, "row", split_axis=0, concat_axis=0, tiled=True).reshape(
        every_adapter * capacity, normalized_input.shape[1]
    )
    delta_rows = jnp.dot(jnp.transpose(placer), returned, preferred_element_type=jnp.float32)
    out_term = jnp.dot(
        attended,
        lax.all_gather(output_projection, "row", axis=1, tiled=True),
        preferred_element_type=jnp.float32,
    )
    own_term = lax.dynamic_slice_in_dim(out_term, first_row, own_count, 0) + delta_rows
    out_term = lax.dynamic_update_slice_in_dim(out_term, own_term, first_row, 0)
    attn_share = lax.psum_scatter(
        out_term.astype(jnp.bfloat16), "col", scatter_dimension=0, tiled=True
    ).astype(jnp.float32)
    residual = (inputs.astype(jnp.float32) + attn_share).astype(jnp.bfloat16)
    whole_mixed = lax.all_gather(residual, "col", axis=0, tiled=True)
    normed_mlp = rms_scaled(whole_mixed.astype(jnp.float32), feed_forward_gain).astype(jnp.bfloat16)

    def add_rows(piece):
        return jnp.dot(normed_mlp, piece, preferred_element_type=jnp.float32)

    gate = add_rows(lax.all_gather(gate_projection, "row", axis=0, tiled=True))
    up_part = add_rows(lax.all_gather(up_projection, "row", axis=0, tiled=True))
    hidden = (jax.nn.silu(gate) * up_part).astype(jnp.bfloat16)
    down_term = jnp.dot(
        hidden,
        lax.all_gather(down_projection, "row", axis=1, tiled=True),
        preferred_element_type=jnp.float32,
    )
    mlp_added = lax.psum_scatter(
        down_term.astype(jnp.bfloat16), "col", scatter_dimension=0, tiled=True
    ).astype(jnp.float32)
    return (residual.astype(jnp.float32) + mlp_added).astype(jnp.bfloat16)


def solution(mesh):
    placed = (
        P(("row", "col"), None),
        P(),
        P("row", None, "col"),
        P(None, None, "col"),
        P("col", "row"),
        P("row", None, "col", None),
        P("row"),
        P("row", None),
        P("row", None),
        P("row", None, None),
        P("row", None, None),
        P(),
        P("row", "col"),
        P("row", "col"),
        P("col", "row"),
    )
    return jax.shard_map(
        on_device, mesh=mesh, in_specs=placed, out_specs=P(("row", "col"), None), check_vma=False
    )
```

profile of v0, /device:TPU:24, one launch (start us, length us, event | category | flops | bytes accessed | tf_op | source)
XLA Modules:
  0.0 407.4 jit_solution(15843340719404520123)
XLA Ops:
  6.5 0.7 all-gather.7.cloned.1.call-update
  7.3 0.7 all-gather.9.cloned.1.call-update
  8.0 0.7 broadcast_subtract_fusion
  8.7 0.1 broadcast_in_dim.106
  8.7 0.1 sub.65
  8.8 1.7 reshape.283
  10.5 0.8 reduce-window.4
  11.4 0.7 fusion.50
  12.1 0.1 fusion.40
  12.2 0.1 reduce_window_sum.18
  12.3 0.1 convert_reduce_fusion
  12.4 0.7 fusion.51
  13.0 0.1 select_reduce_fusion.1
  13.1 0.2 select_reduce_fusion
  13.3 0.7 multiply_add_fusion
  14.0 0.6 broadcast_compare_fusion.2
  14.6 1.4 fusion.58
  16.0 36.5 %all-gather.7.cloned.1.call-done = bf16[512,1792]{1,0:T(8,128)(2,1)} async-done(((bf16[64,1792]{1,0:T(8,128)(2,1)}), bf16[512,1792]{1,0:T(8,128)(2,1)}) %all-gather.7.cloned.1.call-update) | async-done | bytes 1835024 | tf_op jit(solution)/shard_map/all_gather | solution.py:149
  52.5 2.1 fusion
  54.5 0.5 fusion.2
  55.1 0.3 convolution_convert_fusion.2
  55.3 0.9 reshape.286
  56.3 7.4 %all-to-all-start = ((bf16[32,2,2,1792]{3,2,1,0:T(2,128)(2,1)}), bf16[32,2,2,1792]{3,2,1,0:T(2,128)(2,1)S(1)}, u32[]{:S(2)}, u32[]{:S(2)}) async-start(bf16[32,2,2,1792]{3,2,1,0:T(2,128)(2,1)} %reshape.286), calls=%async_computation | async-start | bytes 917504 | tf_op jit(solution)/shard_map/all_to_all | solution.py:184
  63.6 0.6 fusion.49
  64.2 0.8 fusion.57
  65.1 8.1 %all-to-all-done = bf16[32,2,2,1792]{3,2,1,0:T(2,128)(2,1)S(1)} async-done(((bf16[32,2,2,1792]{3,2,1,0:T(2,128)(2,1)}), bf16[32,2,2,1792]{3,2,1,0:T(2,128)(2,1)S(1)}, u32[]{:S(2)}, u32[]{:S(2)}) %all-to-all-start) | async-done | bytes 458784 | tf_op jit(solution)/shard_map/all_to_all | solution.py:184
  73.2 0.7 fusion.7
  73.9 1.2 copy.50
  75.2 5.9 %all-to-all-start.1 = ((bf16[32,2,2,1792]{3,2,1,0:T(2,128)(2,1)}), bf16[32,2,2,1792]{3,2,1,0:T(2,128)(2,1)}, u32[]{:S(2)}, u32[]{:S(2)}) async-start(bf16[32,2,2,1792]{3,2,1,0:T(2,128)(2,1)} %copy.50), calls=%async_computation.1 | async-start | bytes 917504 | tf_op jit(solution)/shard_map/all_to_all | solution.py:191
  81.2 0.7 copy.57
  81.9 0.7 copy.58
  82.6 25.7 %all_gather.23 = bf16[224,1792]{0,1:T(8,128)(2,1)S(1)} all-gather(bf16[224,56]{0,1:T(8,128)(2,1)S(1)} %copy-done.11), channel_id=1, replica_groups=mesh['row'=32,'col'=8] {'row'}, dimensions={1}, use_global_device_ids=true | all-gather | bytes 827904 | tf_op jit(solution)/shard_map/all_gather | solution.py:197
  108.3 0.8 compare_and_fusion
  109.1 2.0 reshape.287
  111.1 3.2 fusion.10
  114.4 0.1 slice_bitcast_fusion.1
  114.6 0.4 copy-done.13
  115.0 0.8 fusion.31
  115.9 0.6 fusion.8
  116.5 0.3 copy-done.7
  116.8 0.5 fusion.9
  117.4 1.0 fusion.13
  118.4 0.8 convolution_bitcast_fusion.1
  119.2 0.1 copy-done.9
  119.3 0.8 fusion.16
  120.1 0.7 fusion.59
  120.8 0.3 copy-done.3
  121.1 0.3 fusion.6
  121.4 1.4 convert_element_type.107
  123.0 37.8 %reduce-scatter.3.cloned.1.call-done = bf16[64,1792]{1,0:T(8,128)(2,1)} async-done(((bf16[512,1792]{1,0:T(8,128)(2,1)}), bf16[64,1792]{1,0:T(8,128)(2,1)}) %reduce-scatter.3.cloned.1.call-update) | async-done | bytes 229392 | tf_op jit(solution)/shard_map/reduce_scatter | solution.py:202
  160.8 1.7 add_convert_fusion.1
  162.5 0.5 all-gather.13.cloned.1.call-update
  163.1 0.5 all-gather.15.cloned.1.call-update
  163.7 0.7 all-gather.17.cloned.1.call-update
  164.4 0.3 reduce-scatter.5.cloned.1.call-start
  164.7 37.3 %all-gather.11.cloned.1.call-done = bf16[512,1792]{1,0:T(8,128)(2,1)} async-done(((bf16[64,1792]{1,0:T(8,128)(2,1)}), bf16[512,1792]{1,0:T(8,128)(2,1)}) %all-gather.11.cloned.1.call-update) | async-done | bytes 1835024 | tf_op jit(solution)/shard_map/all_gather | solution.py:206
  202.0 1.9 fusion.3
  203.9 47.2 %all-gather.13.cloned.1.call-done = bf16[1792,512]{1,0:T(8,128)(2,1)} async-done(((bf16[56,512]{1,0:T(8,128)(2,1)}), bf16[1792,512]{1,0:T(8,128)(2,1)}) %all-gather.13.cloned.1.call-update) | async-done | bytes 1835024 | tf_op jit(solution)/shard_map/all_gather | solution.py:212
  251.1 3.2 fusion.24
  254.3 47.1 %all-gather.15.cloned.1.call-done = bf16[1792,512]{1,0:T(8,128)(2,1)} async-done(((bf16[56,512]{1,0:T(8,128)(2,1)}), bf16[1792,512]{1,0:T(8,128)(2,1)}) %all-gather.15.cloned.1.call-update) | async-done | bytes 1835024 | tf_op jit(solution)/shard_map/all_gather | solution.py:213
  301.4 50.5 %all-gather.17.cloned.1.call-done = bf16[512,1792]{0,1:T(8,128)(2,1)} async-done(((bf16[512,56]{0,1:T(8,128)(2,1)}), bf16[512,1792]{0,1:T(8,128)(2,1)}) %all-gather.17.cloned.1.call-update) | async-done | bytes 1835024 | tf_op jit(solution)/shard_map/all_gather | solution.py:217
  351.8 5.6 %convolution_convert_fusion = bf16[512,1792]{1,0:T(8,128)(2,1)} fusion(bf16[512,1792]{0,1:T(8,128)(2,1)} %all-gather.17.cloned.1.call-done, bf16[1792,512]{1,0:T(8,128)(2,1)} %all-gather.15.cloned.1.call-done, f32[512,512]{1,0:T(8,128)S(1)} %fusion.24, bf16[512,1792]{1,0:T(8,128)(2,1)S(1)} %copy-done.4, f32[1792]{0:T(1024)S(1)} %copy-done.22, ...), kind=kOutput, calls=%fused_computation.10 | convolution fusion | flops 1885208576 | bytes 8397824 | tf_op jit(solution)/shard_map/dot_general | solution.py:215
  357.5 41.4 %reduce-scatter.5.cloned.1.call-done = bf16[64,1792]{1,0:T(8,128)(2,1)} async-done(((bf16[512,1792]{1,0:T(8,128)(2,1)}), bf16[64,1792]{1,0:T(8,128)(2,1)}) %reduce-scatter.5.cloned.1.call-update) | async-done | bytes 229392 | tf_op jit(solution)/shard_map/reduce_scatter | solution.py:220
  398.8 1.7 add_convert_fusion
  (62 shorter events, 0.5 us)
Async XLA Ops:
  6.5 66.6 %copy-start = (bf16[2,16,1792]{2,1,0:T(8,128)(2,1)S(1)}, bf16[2,16,1792]{2,1,0:T(8,128)(2,1)}, u32[]{:S(2)}) copy-start(bf16[2,16,1792]{2,1,0:T(8,128)(2,1)} %param.25) | copy-start | bytes 344068
  6.5 48.0 %copy-start.12 = (f32[1792]{0:T(1024)S(1)}, f32[1792]{0:T(1024)}, u32[]{:S(2)}) copy-start(f32[1792]{0:T(1024)} %param.16) | copy-start | bytes 21508
  6.5 45.9 %all-gather.7.cloned.1.call-start = ((), (), s32[]{:S(2)}) async-start(), calls=%async_computation.4 | async-start | bytes 2064384 | tf_op jit(solution)/shard_map/all_gather | solution.py:149
  7.3 103.8 %all-gather.9.cloned.1.call-start = ((), (), s32[]{:S(2)}) async-start(), calls=%async_computation.5 | async-start | bytes 2838528 | tf_op jit(solution)/shard_map/all_gather | solution.py:157
  52.5 2.1 copy-start.1
  55.0 18.1 %copy-start.10 = (bf16[2,1792,16]{1,2,0:T(8,128)(2,1)S(1)}, bf16[2,1792,16]{1,2,0:T(8,128)(2,1)}, u32[]{:S(2)}) copy-start(bf16[2,1792,16]{1,2,0:T(8,128)(2,1)} %param.24) | copy-start | bytes 344068
  56.3 16.9 %all-to-all-start = ((bf16[32,2,2,1792]{3,2,1,0:T(2,128)(2,1)}), bf16[32,2,2,1792]{3,2,1,0:T(2,128)(2,1)S(1)}, u32[]{:S(2)}, u32[]{:S(2)}) async-start(bf16[32,2,2,1792]{3,2,1,0:T(2,128)(2,1)} %reshape.286), calls=%async_computation | async-start | bytes 917504 | tf_op jit(solution)/shard_map/all_to_all | solution.py:184
  65.1 16.1 %copy-start.6 = (bf16[8,1,2,64,112]{4,3,2,1,0:T(8,128)(2,1)S(1)}, bf16[8,1,2,64,112]{4,3,2,1,0:T(8,128)(2,1)}, u32[]{:S(2)}) copy-start(bf16[8,1,2,64,112]{4,3,2,1,0:T(8,128)(2,1)} %get-tuple-element.14) | copy-start | bytes 688132
  65.1 16.8 %copy-start.5 = (bf16[8,1,2,64,112]{4,3,2,1,0:T(8,128)(2,1)S(1)}, bf16[8,1,2,64,112]{4,3,2,1,0:T(8,128)(2,1)}, u32[]{:S(2)}) copy-start(bf16[8,1,2,64,112]{4,3,2,1,0:T(8,128)(2,1)} %get-tuple-element.13) | copy-start | bytes 688132
  65.1 17.5 %copy-start.11 = (bf16[224,56]{0,1:T(8,128)(2,1)S(1)}, bf16[224,56]{0,1:T(8,128)(2,1)}, u32[]{:S(2)}) copy-start(bf16[224,56]{0,1:T(8,128)(2,1)} %param.19) | copy-start | bytes 75268
  73.9 34.4 %copy-start.21 = (pred[512]{0:T(512)(128)(4,1)S(1)}, pred[512]{0:T(512)(128)(4,1)}, u32[]{:S(2)}) copy-start(pred[512]{0:T(512)(128)(4,1)} %fusion.49) | copy-start | bytes 1540
  75.2 34.0 %all-to-all-start.1 = ((bf16[32,2,2,1792]{3,2,1,0:T(2,128)(2,1)}), bf16[32,2,2,1792]{3,2,1,0:T(2,128)(2,1)}, u32[]{:S(2)}, u32[]{:S(2)}) async-start(bf16[32,2,2,1792]{3,2,1,0:T(2,128)(2,1)} %copy.50), calls=%async_computation.1 | async-start | bytes 917504 | tf_op jit(solution)/shard_map/all_to_all | solution.py:191
  81.1 79.7 %reduce-scatter.3.cloned.1.call-start = ((), (), s32[]{:S(2)}) async-start(), calls=%async_computation.6 | async-start | bytes 2064384 | tf_op jit(solution)/shard_map/reduce_scatter | solution.py:202
  114.3 0.7 copy-start.13
  114.3 0.7 copy-start.14
  114.3 0.7 copy-start.15
  114.3 0.7 copy-start.16
  114.4 0.7 copy-start.17
  114.4 0.7 copy-start.18
  114.4 0.7 copy-start.19
  114.4 0.7 copy-start.20
  115.9 1.0 copy-start.7
  118.4 1.0 copy-start.9
  120.1 1.0 copy-start.3
  121.4 39.3 %copy-start.8 = (bf16[64,1792]{1,0:T(8,128)(2,1)S(1)}, bf16[64,1792]{1,0:T(8,128)(2,1)}, u32[]{:S(2)}) copy-start(bf16[64,1792]{1,0:T(8,128)(2,1)} %param.15) | copy-start | bytes 688132
  122.9 128.2 %copy-start.22 = (f32[1792]{0:T(1024)S(1)}, f32[1792]{0:T(1024)}, u32[]{:S(2)}) copy-start(f32[1792]{0:T(1024)} %param.26) | copy-start | bytes 21508
  122.9 79.1 %all-gather.11.cloned.1.call-start = ((), (), s32[]{:S(2)}) async-start(), calls=%async_computation.7 | async-start | bytes 2064384 | tf_op jit(solution)/shard_map/all_gather | solution.py:206
  162.5 88.6 %all-gather.13.cloned.1.call-start = ((), (), s32[]{:S(2)}) async-start(), calls=%async_computation.8 | async-start | bytes 1892352 | tf_op jit(solution)/shard_map/all_gather | solution.py:212
  163.1 138.3 %all-gather.15.cloned.1.call-start = ((), (), s32[]{:S(2)}) async-start(), calls=%async_computation.9 | async-start | bytes 1892352 | tf_op jit(solution)/shard_map/all_gather | solution.py:213
  163.6 188.2 %all-gather.17.cloned.1.call-start = ((), (), s32[]{:S(2)}) async-start(), calls=%async_computation.10 | async-start | bytes 1892352 | tf_op jit(solution)/shard_map/all_gather | solution.py:217
  164.4 234.5 %reduce-scatter.5.cloned.1.call-start = ((), (), s32[]{:S(2)}) async-start(), calls=%async_computation.11 | async-start | bytes 2064384 | tf_op jit(solution)/shard_map/reduce_scatter | solution.py:220
  203.9 147.9 %copy-start.4 = (bf16[512,1792]{1,0:T(8,128)(2,1)S(1)}, bf16[512,1792]{1,0:T(8,128)(2,1)}, u32[]{:S(2)}) copy-start(bf16[512,1792]{1,0:T(8,128)(2,1)} %all-gather.11.cloned.1.call-done) | copy-start | bytes 5505028
  254.3 144.6 %copy-start.2 = (bf16[64,1792]{1,0:T(8,128)(2,1)S(1)}, bf16[64,1792]{1,0:T(8,128)(2,1)}, u32[]{:S(2)}) copy-start(bf16[64,1792]{1,0:T(8,128)(2,1)} %add_convert_fusion.1) | copy-start | bytes 688132
Sparse Core Ops, SparseCore 0:
  9.1 43.2 all-gather.6
  55.1 48.2 all-gather.8
  123.0 37.6 reduce-scatter.2
  162.6 39.3 all-gather.10
  204.3 46.6 all-gather.12
  253.5 47.8 all-gather.14
  303.9 47.8 all-gather.16
  357.6 41.2 reduce-scatter.4
where the time goes:
time: 408 us; the launch traced here: 407 us
  waiting for transfers between devices  309 us (76%)
  blocking collectives  25.7 us (6%)
  matrix products  16.7 us (4%)
  other arithmetic  16.4 us (4%)
  starting transfers between devices  13.8 us (3%)
  between operations  13.8 us (3%)
  local copies, waits for them, and re-layouts  11.8 us (3%)
    all_gather x1, waiting for transfers between devices, on_device(): lax.all_gather(down_projection, 'row', axis=1, tiled=True)  50.5 us
    all_gather x1, waiting for transfers between devices, on_device(): gate = add_rows(lax.all_gather(gate_projection, 'row', axis=0, tiled=True))  47.2 us
    all_gather x1, waiting for transfers between devices, on_device(): up_part = add_rows(lax.all_gather(up_projection, 'row', axis=0, tiled=True))  47.1 us
    reduce_scatter x1, waiting for transfers between devices, on_device(): lax.psum_scatter(down_term.astype(jnp.bfloat16), 'col', scatter_dimension...  41.4 us
    reduce_scatter x1, waiting for transfers between devices, on_device(): lax.psum_scatter(out_term.astype(jnp.bfloat16), 'col', scatter_dimension=...  37.8 us
    all_gather x1, waiting for transfers between devices, on_device(): whole_mixed = lax.all_gather(residual, 'col', axis=0, tiled=True)  37.3 us
    all_gather x1, waiting for transfers between devices, on_device(): gathered = lax.all_gather(inputs, 'col', axis=0, tiled=True)  36.5 us
    all_gather x1, blocking collectives, on_device(): lax.all_gather(output_projection, 'row', axis=1, tiled=True)  25.7 us
  transfers between devices with their start and end apart: 10, of which 8 were waited for; matrix products, arithmetic and copies ran while one was open for 6% of the time, Pallas kernels for 0%

commit v1 on v0

v1 whole, which is shorter than its diff:
```python
import functools

import jax
import jax.numpy as jnp
from jax import lax
from jax.experimental import pallas as pl
from jax.experimental.pallas import tpu as pltpu
from jax.sharding import PartitionSpec as P

HD = 112


epsilon = 1e-05


def rms_scaled(values, gain_row):
    mean_square = jnp.mean(values * values, axis=-1, keepdims=True)
    return values * lax.rsqrt(mean_square + epsilon) * gain_row


MESH = pl.DeviceIdType.MESH
NX, NY, NC = 4, 4, 2
ANY = pl.BlockSpec(memory_space=pl.ANY)
VMEM = pl.BlockSpec(memory_space=pltpu.VMEM)


def remote(source, target, send, recv, row, col):
    return pltpu.make_async_remote_copy(
        src_ref=source,
        dst_ref=target,
        send_sem=send,
        recv_sem=recv,
        device_id=(row, col),
        device_id_type=MESH,
    )


class Place:
    def __init__(self):
        self.row = lax.axis_index("row")
        self.z = lax.axis_index("col")
        self.count = lax.axis_size("col")
        self.row_count = lax.axis_size("row")
        self.c = lax.rem(self.row, NC)
        self.y = lax.rem(lax.div(self.row, NC), NY)
        self.x = lax.div(self.row, NC * NY)

    def col_at(self, offset):
        return lax.rem(self.z + offset + self.count, self.count)

    def x_at(self, offset):
        return lax.rem(self.x + offset + NX, NX)

    def y_at(self, offset):
        return lax.rem(self.y + offset + NY, NY)

    def row_of(self, x, y, c):
        return (x * NY + y) * NC + c

    def row_at(self, offset):
        return lax.rem(self.row + offset, self.row_count)

    def greet(self, reach):
        peers = [(self.row, self.col_at(1)), (self.row, self.col_at(-1))]
        if reach == "plane":
            for offset in range(1, NX):
                peers.append((self.row_of(self.x_at(offset), self.y, self.c), self.z))
            for offset in range(1, NY):
                peers.append((self.row_of(self.x, self.y_at(offset), self.c), self.z))
            peers.append((self.row_of(self.x, self.y, 1 - self.c), self.z))
        if reach == "row":
            for offset in range(1, self.row_count):
                peers.append((self.row_at(offset), self.z))
        barrier = pltpu.get_barrier_semaphore()
        for peer in peers:
            pl.semaphore_signal(barrier, inc=1, device_id=peer, device_id_type=MESH)
        return barrier, len(peers)


class RingGather:
    def __init__(self, place, own, whole, sends, recvs):
        self.place, self.own, self.whole = place, own, whole
        self.sends, self.recvs = sends, recvs
        self.hops = place.count // 2
        self.half = own.shape[0] // 2
        self.copies = {}

    def hop(self, k):
        place = self.place
        for u in range(2):
            for way in range(2):
                if k == self.hops - 1 and u != way:
                    continue
                if k > 0:
                    self.copies[k - 1, way, u].wait_recv()
                origin = place.col_at(-k if way == 0 else k)
                rows = pl.ds(u * self.half, self.half)
                source = self.own.at[rows] if k == 0 else self.whole.at[origin, rows]
                copy = remote(
                    source,
                    self.whole.at[origin, rows],
                    self.sends.at[k, way, u],
                    self.recvs.at[k, way, u],
                    place.row,
                    place.col_at(1 if way == 0 else -1),
                )
                copy.start()
                self.copies[k, way, u] = copy

    def finish(self):
        last = self.hops - 1
        for (k, way, u), copy in self.copies.items():
            copy.wait_send()
            if k == last or (k == last - 1 and u != way):
                copy.wait_recv()


class PlaneGather:
    def __init__(self, place, own, whole, cut, sends, recvs, local):
        self.place, self.own, self.whole = place, own, whole
        self.lanes = (pl.ds(0, cut), pl.ds(cut, own.shape[1] - cut))
        self.sends, self.recvs = sends, recvs
        self.local = pltpu.make_async_copy(own, whole.at[place.x, place.y, place.c], local)
        self.first, self.second, self.sibling = {}, {}, {}

    def group(self, path, offset):
        place, lanes = self.place, self.lanes[path]
        if path == 0:
            return self.whole.at[:, place.y_at(-offset), place.c, :, lanes]
        return self.whole.at[place.x_at(-offset), :, place.c, :, lanes]

    def peer(self, along_x, offset):
        place = self.place
        if along_x:
            return place.row_of(place.x_at(offset), place.y, place.c)
        return place.row_of(place.x, place.y_at(offset), place.c)

    def start(self):
        place = self.place
        self.local.start()
        for offset in range(1, 4):
            for path in range(2):
                lanes = self.lanes[path]
                copy = remote(
                    self.own.at[:, lanes],
                    self.whole.at[place.x, place.y, place.c, :, lanes],
                    self.sends.at[path, 0, offset],
                    self.recvs.at[path, 0, offset],
                    self.peer(path == 0, offset),
                    place.z,
                )
                copy.start()
                self.first[path, offset] = copy

    def hand_over(self, path, offset):
        place = self.place
        copy = remote(
            self.group(path, offset),
            self.group(path, offset),
            self.sends.at[path, 2, offset],
            self.recvs.at[path, 2, offset],
            place.row_of(place.x, place.y, 1 - place.c),
            place.z,
        )
        copy.start()
        self.sibling[path, offset] = copy

    def spread(self):
        self.local.wait()
        for path in range(2):
            for offset in range(1, 4):
                self.first[path, offset].wait_recv()
            for offset in range(1, 4):
                copy = remote(
                    self.group(path, 0),
                    self.group(path, 0),
                    self.sends.at[path, 1, offset],
                    self.recvs.at[path, 1, offset],
                    self.peer(path == 1, offset),
                    self.place.z,
                )
                copy.start()
                self.second[path, offset] = copy
            self.hand_over(path, 0)

    def share(self):
        for offset in range(1, 4):
            for path in range(2):
                self.second[path, offset].wait_recv()
                self.hand_over(path, offset)

    def finish(self):
        for copy in self.sibling.values():
            copy.wait_recv()
        for group in (self.first, self.second, self.sibling):
            for copy in group.values():
                copy.wait_send()


class RingSum:
    def __init__(self, place, part, stage, land_half, land, sends, recvs):
        self.place, self.part, self.stage = place, part, stage
        self.land_half, self.land, self.sends, self.recvs = land_half, land, sends, recvs
        self.hops = place.count // 2
        self.half = part.shape[1] // 2
        self.cols = part.shape[2] // 2
        self.copies = {}

    def hop(self, k):
        place, half = self.place, self.half
        for h in range(2):
            cols = pl.ds(h * self.cols, self.cols)
            for way in range(2):
                left = self.hops - k
                block = place.col_at(left if way == 0 else -left)
                if k == 0:
                    source = self.part.at[block, pl.ds(way * half, half), cols]
                    target = self.land_half.at[way, h]
                else:
                    self.copies[k - 1, way, h].wait_recv()
                    stage = self.stage.at[k - 1, way, h]
                    if k == 1:
                        got = pl.ds(way * half, half)
                        rest = pl.ds((1 - way) * half, half)
                        stage[got] = (
                            self.part[block, got, cols].astype(jnp.float32)
                            + self.land_half[way, h].astype(jnp.float32)
                        ).astype(jnp.bfloat16)
                        stage[rest] = self.part[block, rest, cols]
                    else:
                        stage[...] = (
                            self.part[block, :, cols].astype(jnp.float32)
                            + self.land[k - 2, way, h].astype(jnp.float32)
                        ).astype(jnp.bfloat16)
                    source = stage
                    target = self.land.at[k - 1, way, h]
                copy = remote(
                    source,
                    target,
                    self.sends.at[k, way, h],
                    self.recvs.at[k, way, h],
                    place.row,
                    place.col_at(1 if way == 0 else -1),
                )
                copy.start()
                self.copies[k, way, h] = copy

    def total(self, h):
        last = self.hops - 1
        for way in range(2):
            self.copies[last, way, h].wait_recv()
        cols = pl.ds(h * self.cols, self.cols)
        return (
            self.part[self.place.z, :, cols].astype(jnp.float32)
            + self.land[last - 1, 0, h].astype(jnp.float32)
            + self.land[last - 1, 1, h].astype(jnp.float32)
        )

    def finish(self):
        for copy in self.copies.values():
            copy.wait_send()


def ring_sum_scratch(count, block_rows, width):
    hops = count // 2
    return [
        pltpu.VMEM((hops - 1, 2, 2, block_rows, width // 2), jnp.bfloat16),
        pltpu.VMEM((2, 2, block_rows // 2, width // 2), jnp.bfloat16),
        pltpu.VMEM((hops - 1, 2, 2, block_rows, width // 2), jnp.bfloat16),
    ] + ring_semaphores(count)


def ring_semaphores(count):
    return [pltpu.SemaphoreType.DMA((count // 2, 2, 2)), pltpu.SemaphoreType.DMA((count // 2, 2, 2))]


def plane_semaphores():
    return [
        pltpu.SemaphoreType.DMA((2, 3, 4)),
        pltpu.SemaphoreType.DMA((2, 3, 4)),
        pltpu.SemaphoreType.DMA,
    ]


class Exchange:
    def __init__(self, place, outgoing, incoming, send, recv):
        self.place, self.outgoing, self.incoming = place, outgoing, incoming
        self.send, self.recv = send, recv

    def start(self):
        place = self.place
        for offset in range(1, place.row_count):
            peer = place.row_at(offset)
            remote(
                self.outgoing.at[peer],
                self.incoming.at[place.row],
                self.send,
                self.recv,
                peer,
                place.z,
            ).start()
        self.incoming[place.row] = self.outgoing[place.row]

    def all_but_one(self, ref, semaphore):
        blocks = ref.at[pl.ds(0, self.place.row_count - 1)]
        return pltpu.make_async_copy(blocks, blocks, semaphore)

    def arrived(self):
        self.all_but_one(self.incoming, self.recv).wait()

    def finish(self):
        self.all_but_one(self.outgoing, self.send).wait()


def placer_of(ids_col, capacity, slots):
    count = ids_col.shape[0]
    down = lax.broadcasted_iota(jnp.int32, (count, count), 0)
    across = lax.broadcasted_iota(jnp.int32, (count, count), 1)
    ids_row = jnp.sum(jnp.where(down == across, ids_col, 0), axis=0, keepdims=True)
    same_before = (ids_col == ids_row) & (down < across)
    rank = jnp.sum(same_before.astype(jnp.int32), axis=0, keepdims=True)
    target = ids_row * capacity + rank
    slot = lax.broadcasted_iota(jnp.int32, (slots, count), 0)
    return jnp.where(slot == target, 1.0, 0.0).astype(jnp.bfloat16)


def open_body(
    cut, capacity, own, own_hbm, gain, ids, down_map, up_map, weights, tokens, base, weight_rows, *scratch
):
    place = Place()
    ring = RingGather(place, own_hbm, tokens, scratch[0], scratch[1])
    plane = PlaneGather(place, weights, weight_rows, cut, scratch[2], scratch[3], scratch[4])
    kept = pltpu.make_async_copy(own_hbm, tokens.at[place.z], scratch[5])
    asked, asking, answer, answered = scratch[6:10]
    there = Exchange(place, asked, asking, scratch[10], scratch[11])
    back = Exchange(place, answer, answered, scratch[12], scratch[13])
    own_count, width = own.shape
    rows, per_row, _ = asked.shape
    slots = rows * per_row

    met = place.greet("row")
    own_rows = rms_scaled(own[...].astype(jnp.float32), gain[...]).astype(jnp.bfloat16)
    first_row = pl.multiple_of(place.z * own_count, own_count)
    placer = placer_of(ids[pl.ds(first_row, own_count), :], capacity, slots)
    outgoing = jnp.dot(placer, own_rows, preferred_element_type=jnp.float32)
    asked[...] = outgoing.reshape(rows, per_row, width).astype(jnp.bfloat16)
    pl.semaphore_wait(*met)
    ring.hop(0)
    plane.start()
    there.start()
    kept.start()
    plane.spread()
    ring.hop(1)

    there.arrived()
    received = asking[...].reshape(slots, width)
    slot = lax.broadcasted_iota(jnp.int32, (slots, 1), 0)
    adapter = lax.rem(lax.div(slot, capacity), down_map.shape[0])
    result = jnp.zeros((slots, width), jnp.float32)
    for kept_one in range(down_map.shape[0]):
        low = jnp.dot(received, down_map[kept_one], preferred_element_type=jnp.float32)
        low = jnp.where(adapter == kept_one, low, 0.0).astype(jnp.bfloat16)
        result = result + jnp.dot(low, up_map[kept_one], preferred_element_type=jnp.float32)
    answer[...] = result.reshape(rows, per_row, width).astype(jnp.bfloat16)
    back.start()

    ring.hop(2)
    plane.share()
    ring.hop(3)
    back.arrived()
    base[...] = own[...].astype(jnp.float32) + lax.dot_general(
        placer,
        answered[...].reshape(slots, width),
        (((0,), (0,)), ((), ())),
        preferred_element_type=jnp.float32,
    )
    kept.wait()
    there.finish()
    back.finish()
    ring.finish()
    plane.finish()


def attend_body(
    lengths, valid, tokens, gain, weights, taps, cache, out, normed, mixed, attended
):
    tok_count = tokens.shape[0]
    heads_wide = attended.shape[1]
    requests, _, head_count, window, head = cache.shape
    for lower in range(0, tok_count, 128):
        rows = pl.ds(lower, 128)
        normed[rows] = rms_scaled(tokens[rows].astype(jnp.float32), gain[...]).astype(jnp.bfloat16)
    mixed[...] = jnp.dot(normed[...], weights[...], preferred_element_type=jnp.float32)

    spot = lax.broadcasted_iota(jnp.int32, (tok_count, 1), 0)
    segment = jnp.zeros((tok_count, 1), jnp.int32)
    begin = jnp.zeros((tok_count, 1), jnp.int32)
    finish = 0
    for request in range(requests):
        finish = finish + lengths[0, request]
        past = spot >= finish
        segment = segment + past.astype(jnp.int32)
        begin = jnp.where(past, finish, begin)
    held = jnp.zeros((tok_count, 1), jnp.int32)
    for request in range(requests):
        held = jnp.where(segment == request, valid[0, request], held)
    inside = spot - begin
    first_key = jnp.maximum(begin, spot - (window - 1))
    first_slot = segment * window + jnp.maximum(window - held, inside + 1)
    last_slot = segment * window + (window - 1)

    def convolved(values, which):
        total = taps[0, which : which + 1, :] * values
        for offset in range(1, taps.shape[0]):
            moved = jnp.where(inside >= offset, pltpu.roll(values, offset, 0), 0.0)
            total = total + taps[offset, which : which + 1, :] * moved
        return total

    queries = mixed[:, heads_wide : 2 * heads_wide].astype(jnp.bfloat16)
    keys_used = convolved(mixed[:, 2 * heads_wide : 3 * heads_wide], 0).astype(jnp.bfloat16)
    raw_values = mixed[:, 3 * heads_wide :]
    values_used = (raw_values * jax.nn.sigmoid(convolved(raw_values, 1))).astype(jnp.bfloat16)

    scale = head ** (-0.5)
    step = 128
    both = (((1,), (1,)), ((), ()))
    for lower in range(0, tok_count, step):
        upper = lower + step
        start = max(0, lower - window)
        key_spot = start + lax.broadcasted_iota(jnp.int32, (step, upper - start), 1)
        near = (key_spot <= spot[lower:upper]) & (key_spot >= first_key[lower:upper])
        slot = lax.broadcasted_iota(jnp.int32, (step, requests * window), 1)
        cached = (slot >= first_slot[lower:upper]) & (slot <= last_slot[lower:upper])
        pieces = []
        for h in range(head_count):
            cols = slice(h * head, (h + 1) * head)
            query = queries[lower:upper, cols]
            near_scores = scale * lax.dot_general(
                query, keys_used[start:upper, cols], both, preferred_element_type=jnp.float32
            )
            cached_scores = scale * lax.dot_general(
                query,
                cache[:, 0, h].reshape(requests * window, head),
                both,
                preferred_element_type=jnp.float32,
            )
            near_scores = jnp.where(near, near_scores, -jnp.inf)
            cached_scores = jnp.where(cached, cached_scores, -jnp.inf)
            most = jnp.maximum(
                jnp.max(near_scores, axis=-1, keepdims=True),
                jnp.max(cached_scores, axis=-1, keepdims=True),
            )
            near_exp = jnp.exp(near_scores - most)
            cached_exp = jnp.exp(cached_scores - most)
            total = jnp.sum(near_exp, axis=-1, keepdims=True) + jnp.sum(
                cached_exp, axis=-1, keepdims=True
            )
            inverse = 1.0 / total
            pieces.append(
                jnp.dot(
                    (near_exp * inverse).astype(jnp.bfloat16),
                    values_used[start:upper, cols],
                    preferred_element_type=jnp.float32,
                )
                + jnp.dot(
                    (cached_exp * inverse).astype(jnp.bfloat16),
                    cache[:, 1, h].reshape(requests * window, head),
                    preferred_element_type=jnp.float32,
                )
            )
        attended[lower:upper, :] = jnp.concatenate(pieces, axis=1).astype(jnp.bfloat16)
    out[...] = lax.dot_general(
        attended[...], weights[:, :heads_wide], both, preferred_element_type=jnp.float32
    ).astype(jnp.bfloat16)


def feed_body(tokens, gain, weights, out, normed):
    tok_count = tokens.shape[0]
    hidden_count = weights.shape[1] // 3
    for lower in range(0, tok_count, 128):
        rows = pl.ds(lower, 128)
        normed[rows] = rms_scaled(tokens[rows].astype(jnp.float32), gain[...]).astype(jnp.bfloat16)
    gate = jnp.dot(normed[...], weights[:, :hidden_count], preferred_element_type=jnp.float32)
    up_part = jnp.dot(
        normed[...], weights[:, hidden_count : 2 * hidden_count], preferred_element_type=jnp.float32
    )
    hidden = (jax.nn.silu(gate) * up_part).astype(jnp.bfloat16)
    out[...] = lax.dot_general(
        hidden,
        weights[:, 2 * hidden_count :],
        (((1,), (1,)), ((), ())),
        preferred_element_type=jnp.float32,
    ).astype(jnp.bfloat16)


def middle_body(cut, part, base, weights, tokens, residual, weight_rows, *scratch):
    place = Place()
    sums = RingSum(place, part, *scratch[0:5])
    ring = RingGather(place, residual, tokens, scratch[5], scratch[6])
    plane = PlaneGather(place, weights, weight_rows, cut, scratch[7], scratch[8], scratch[9])
    kept = pltpu.make_async_copy(residual, tokens.at[place.z], scratch[10])
    pl.semaphore_wait(*place.greet("plane"))
    sums.hop(0)
    plane.start()
    sums.hop(1)
    plane.spread()
    sums.hop(2)
    sums.hop(3)
    for h in range(2):
        cols = pl.ds(h * sums.cols, sums.cols)
        residual[:, cols] = (base[:, cols] + sums.total(h)).astype(jnp.bfloat16)
    ring.hop(0)
    kept.start()
    plane.share()
    ring.hop(1)
    ring.hop(2)
    ring.hop(3)
    kept.wait()
    sums.finish()
    ring.finish()
    plane.finish()


def close_body(part, base, out, *scratch):
    place = Place()
    sums = RingSum(place, part, *scratch)
    pl.semaphore_wait(*place.greet("ring"))
    for k in range(sums.hops):
        sums.hop(k)
    for h in range(2):
        cols = pl.ds(h * sums.cols, sums.cols)
        out[:, cols] = (base[:, cols].astype(jnp.float32) + sums.total(h)).astype(jnp.bfloat16)
    sums.finish()


def params(number):
    return pltpu.CompilerParams(
        collective_id=number, has_side_effects=True, vmem_limit_bytes=40 * 1024 * 1024
    )


def open_exchange(own, gain, ids, down_map, up_map, weights, count, rows):
    block_rows, width = own.shape
    weight_rows, lanes = weights.shape
    kept_count = down_map.shape[0]
    capacity = max(2, 2 * block_rows // (kept_count * rows))
    slots = pltpu.VMEM((rows, kept_count * capacity, width), jnp.bfloat16)
    return pl.pallas_call(
        functools.partial(open_body, lanes // 256 * 128, capacity),
        out_shape=(
            jax.ShapeDtypeStruct((count, block_rows, width), jnp.bfloat16),
            jax.ShapeDtypeStruct((block_rows, width), jnp.float32),
            jax.ShapeDtypeStruct((NX, NY, NC, weight_rows, lanes), jnp.bfloat16),
        ),
        in_specs=[VMEM, ANY, VMEM, VMEM, VMEM, VMEM, ANY],
        out_specs=(ANY, VMEM, ANY),
        scratch_shapes=ring_semaphores(count)
        + plane_semaphores()
        + [pltpu.SemaphoreType.DMA, slots, slots, slots, slots]
        + [pltpu.SemaphoreType.DMA] * 4,
        compiler_params=params(0),
        cost_estimate=pl.CostEstimate(flops=0, bytes_accessed=60_000_000, transcendentals=0),
        name="gather_tokens_and_weights",
    )(own, own, gain, ids, down_map, up_map, weights)


def attention(lengths, valid, tokens, gain, weights, taps, cache):
    tok_count, width = tokens.shape
    lanes = weights.shape[1]
    scalars = pl.BlockSpec(memory_space=pltpu.SMEM)
    return pl.pallas_call(
        attend_body,
        out_shape=jax.ShapeDtypeStruct((tok_count, width), jnp.bfloat16),
        in_specs=[scalars, scalars] + [VMEM] * 5,
        out_specs=VMEM,
        scratch_shapes=[
            pltpu.VMEM((tok_count, width), jnp.bfloat16),
            pltpu.VMEM((tok_count, lanes), jnp.float32),
            pltpu.VMEM((tok_count, lanes // 4), jnp.bfloat16),
        ],
        compiler_params=pltpu.CompilerParams(vmem_limit_bytes=48 * 1024 * 1024),
        name="attention",
    )(lengths, valid, tokens, gain, weights, taps, cache)


def feed_forward(tokens, gain, weights):
    tok_count, width = tokens.shape
    return pl.pallas_call(
        feed_body,
        out_shape=jax.ShapeDtypeStruct((tok_count, width), jnp.bfloat16),
        in_specs=[VMEM] * 3,
        out_specs=VMEM,
        scratch_shapes=[pltpu.VMEM((tok_count, width), jnp.bfloat16)],
        compiler_params=pltpu.CompilerParams(vmem_limit_bytes=48 * 1024 * 1024),
        name="feed_forward",
    )(tokens, gain, weights)


def middle_exchange(part, base, weights):
    count, block_rows, width = part.shape
    weight_rows, lanes = weights.shape
    return pl.pallas_call(
        functools.partial(middle_body, lanes // 256 * 128),
        out_shape=(
            jax.ShapeDtypeStruct((count, block_rows, width), jnp.bfloat16),
            jax.ShapeDtypeStruct((block_rows, width), jnp.bfloat16),
            jax.ShapeDtypeStruct((NX, NY, NC, weight_rows, lanes), jnp.bfloat16),
        ),
        in_specs=[VMEM, VMEM, ANY],
        out_specs=(ANY, VMEM, ANY),
        scratch_shapes=ring_sum_scratch(count, block_rows, width)
        + ring_semaphores(count)
        + plane_semaphores()
        + [pltpu.SemaphoreType.DMA],
        compiler_params=params(1),
        cost_estimate=pl.CostEstimate(flops=0, bytes_accessed=100_000_000, transcendentals=0),
        name="sum_then_gather",
    )(part, base, weights)


def close_exchange(part, base):
    count, block_rows, width = part.shape
    return pl.pallas_call(
        close_body,
        out_shape=jax.ShapeDtypeStruct((block_rows, width), jnp.bfloat16),
        in_specs=[VMEM, VMEM],
        out_specs=VMEM,
        scratch_shapes=ring_sum_scratch(count, block_rows, width),
        compiler_params=params(2),
        cost_estimate=pl.CostEstimate(flops=0, bytes_accessed=50_000_000, transcendentals=0),
        name="sum_hidden_units",
    )(part, base)


def on_device(
    inputs,
    attention_norm_gain,
    query_key_value_weight,
    filter_taps,
    output_projection,
    window_key_value,
    cache_valid_length,
    lengths,
    token_adapter_index,
    adapter_down_map,
    adapter_up_map,
    feed_forward_gain,
    gate_projection,
    up_projection,
    down_projection,
):
    own_count, width = inputs.shape
    row_count = lax.axis_size("row")
    col_count = lax.axis_size("col")
    tok_count = col_count * own_count
    head_cols = filter_taps.shape[2]
    qkv_rows = query_key_value_weight.shape[0]

    first_weights = jnp.concatenate(
        [
            jnp.transpose(output_projection),
            query_key_value_weight.reshape(qkv_rows, 3 * head_cols),
        ],
        axis=1,
    )
    later_weights = jnp.concatenate(
        [gate_projection, up_projection, jnp.transpose(down_projection)], axis=1
    )
    gathered, base, first_rows = open_exchange(
        inputs,
        attention_norm_gain[None, :],
        token_adapter_index,
        adapter_down_map,
        adapter_up_map,
        first_weights,
        col_count,
        row_count,
    )
    requests, _, heads, merged = window_key_value.shape
    out_term = attention(
        lengths,
        cache_valid_length[None, :],
        gathered.reshape(tok_count, width),
        attention_norm_gain[None, :],
        first_rows.reshape(width, 4 * head_cols),
        filter_taps,
        window_key_value.reshape(requests, 2, heads, merged // HD, HD),
    )
    whole_mixed, residual, later_rows = middle_exchange(
        out_term.reshape(col_count, own_count, width), base, later_weights
    )
    down_term = feed_forward(
        whole_mixed.reshape(tok_count, width),
        feed_forward_gain[None, :],
        later_rows.reshape(width, 3 * gate_projection.shape[1]),
    )
    return close_exchange(down_term.reshape(col_count, own_count, width), residual)


def solution(mesh):
    placed = (
        P(("row", "col"), None),
        P(),
        P("row", None, "col"),
        P(None, None, "col"),
        P("col", "row"),
        P("row", None, "col", None),
        P("row"),
        P("row", None),
        P("row", None),
        P("row", None, None),
        P("row", None, None),
        P(),
        P("row", "col"),
        P("row", "col"),
        P("col", "row"),
    )
    return jax.shard_map(
        on_device, mesh=mesh, in_specs=placed, out_specs=P(("row", "col"), None), check_vma=False
    )
```

time: 408 us -> 131 us (0.32)
  waiting for transfers between devices: 309 us -> 0 us
  Pallas kernels: 0 us -> 118 us
  blocking collectives: 25.7 us -> 0 us
  matrix products: 16.7 us -> 0 us
  other arithmetic: 16.4 us -> 0.86 us
  starting transfers between devices: 13.8 us -> 0 us
  between operations: 13.8 us -> 0.24 us
    all_gather x6 -> x0, waiting for transfers between devices: 218 us -> none  [the longest x1 50.5 us: on_device(): lax.all_gather(down_projection, 'row', axis=1, tiled=True)]
    pallas_call x0 -> x5, Pallas kernels: none -> 118 us  [the longest x1 46.8 us: middle_exchange(): pl.pallas_call(functools.partial(middle_body, lanes // 256 * 128), out_sh...]
    reduce_scatter x2 -> x0, waiting for transfers between devices: 79.2 us -> none  [the longest x1 41.4 us: on_device(): lax.psum_scatter(down_term.astype(jnp.bfloat16), 'col', scatter_dimension...]
    all_gather x1 -> x0, blocking collectives: 25.7 us -> none  [on_device(): lax.all_gather(output_projection, 'row', axis=1, tiled=True)]
    dot_general x11 -> x0, matrix products: 16.7 us -> none  [the longest x1 5.59 us: on_device(): jnp.dot(hidden, lax.all_gather(down_projection, 'row', axis=1, tiled=True...]
    all_to_all x2 -> x0, starting transfers between devices: 13.3 us -> none  [the longest x1 7.35 us: on_device(): lax.all_to_all(outgoing, 'row', split_axis=0, concat_axis=0, tiled=True)]
    all_to_all x2 -> x0, waiting for transfers between devices: 8.11 us -> none  [the longest x1 8.11 us: on_device(): lax.all_to_all(outgoing, 'row', split_axis=0, concat_axis=0, tiled=True)]
    convert_element_type x6 -> x0, other arithmetic: 6.19 us -> none  [the longest x1 1.68 us: on_device(): residual = (inputs.astype(jnp.float32) + attn_share).astype(jnp.bfloat16)]
  transfers between devices with their start and end apart: 10 -> 0, of which waited for: 8 -> 0; matrix products, arithmetic and copies ran while one was open for 6% -> 0% of each run, Pallas kernels for 0% -> 0%
where the time goes in v1:
time: 131 us; the launch traced here: 130 us
  Pallas kernels  118 us (90%)
  local copies, waits for them, and re-layouts  11.3 us (9%)
    pallas_call x1, Pallas kernels, middle_exchange(): pl.pallas_call(functools.partial(middle_body, lanes // 256 * 128), out_sh...  46.8 us
    pallas_call x1, Pallas kernels, open_exchange(): pl.pallas_call(functools.partial(open_body, lanes // 256 * 128, capacity)...  33.1 us
    pallas_call x1, Pallas kernels, close_exchange(): pl.pallas_call(close_body, out_shape=jax.ShapeDtypeStruct((block_rows, wi...  22.1 us
    pallas_call x1, Pallas kernels, attention(): pl.pallas_call(attend_body, out_shape=jax.ShapeDtypeStruct((tok_count, wi...  9.45 us
    unnamed x30, local copies, waits for them, and re-layouts  8.68 us
    pallas_call x1, Pallas kernels, feed_forward(): pl.pallas_call(feed_body, out_shape=jax.ShapeDtypeStruct((tok_count, widt...  6.06 us

profile of v1, /device:TPU:24, one launch (start us, length us, event | category | flops | bytes accessed | tf_op | source)
XLA Modules:
  0.0 129.9 jit_solution(17340510435592007327)
XLA Ops:
  0.0 0.0 copy-start.2
  0.0 0.0 copy-start.5
  0.0 0.7 broadcast_in_dim.11.gain
  0.8 1.3 %copy.21.down_map = bf16[2,1792,16]{2,1,0:T(8,128)(2,1)S(1)} copy(bf16[2,1792,16]{1,2,0:T(8,128)(2,1)} %param.24) | data formatting | bytes 229376 | tf_op args[9]
  2.1 0.0 copy-start.6
  2.1 0.0 copy-start.7
  2.1 0.0 copy-start.8
  2.1 0.9 copy.19
  3.1 0.1 reshape.24
  3.2 0.8 pad_maximum_fusion.1.weights
  4.0 0.8 copy.20.ids
  4.9 0.0 copy-done.2
  4.9 0.0 copy-done.5
  4.9 33.1 %gather_tokens_and_weights.1 = (bf16[8,64,1792]{2,1,0:T(8,128)(2,1)S(1)}, f32[64,1792]{1,0:T(8,128)S(1)}, bf16[4,4,2,56,896]{4,3,2,1,0:T(8,128)(2,1)S(1)}) custom-call(bf16[64,1792]{1,0:T(8,128)(2,1)S(1)} %copy-done.2, bf16[64,1792]{1,0:T(8,128)(2,1)S(1)} %copy-done.2, f32[1,1792]{1,0:T(1,128)S(1)} %broadcast_in_dim.11.gain, s32[512,1]{1,0:T(8,128)S(1)} %copy.20.ids, ...), custom_call_target="tpu_custom_call" | custom-call | bytes 60000000 | tf_op jit(solution)/shard_map/gather_tokens_and_weights/pallas_call | solution.py:548
  38.0 0.0 copy-start.1
  38.0 1.7 %copy-done.1 = bf16[4,4,2,56,896]{4,3,2,1,0:T(8,128)(2,1)} copy-done((bf16[4,4,2,56,896]{4,3,2,1,0:T(8,128)(2,1)}, bf16[4,4,2,56,896]{4,3,2,1,0:T(8,128)(2,1)S(1)}, u32[]{:S(2)}) %copy-start.1) | copy-done | bytes 3211288
  39.7 0.0 copy-start.3
  39.7 0.8 copy-done.3
  40.5 1.7 %reshape.27.cache = bf16[8,2,2,64,112]{4,3,2,1,0:T(8,128)(2,1)S(1)} reshape(bf16[8,2,2,7168]{3,2,1,0:T(2,128)(2,1)} %param.20) | data formatting | bytes 917504 | tf_op jit(solution)/shard_map/reshape | solution.py:687
  42.2 0.0 copy-done.6
  42.2 0.0 copy-done.7
  42.2 0.0 copy-done.8
  42.2 0.0 copy-start.9
  42.2 0.0 copy-start.10
  42.2 0.0 copy-start.11
  42.2 0.0 copy-start.4
  42.3 9.5 %attention.1 = bf16[512,1792]{1,0:T(8,128)(2,1)S(1)} custom-call(s32[1,8]{1,0:T(1,128)S(1)} %copy-done.7, s32[1,8]{1,0:T(1,128)S(1)} %bitcast.15, bf16[512,1792]{1,0:T(8,128)(2,1)S(1)} %bitcast.14, f32[1,1792]{1,0:T(1,128)S(1)} %broadcast_in_dim.11.gain, bf16[1792,896]{1,0:T(8,128)(2,1)} %bitcast.12, f32[3,2,224]{2,1,0:T(2,128)S(1)} %copy-done.6, ...), custom_call_target="tpu_custom_call" | custom-call | tf_op jit(solution)/shard_map/attention/pallas_call | solution.py:571
  51.7 0.0 copy-start.12
  51.7 0.0 copy-done.9
  51.7 0.0 copy-done.10
  51.7 0.0 copy-done.11
  51.8 0.0 copy-done.4
  51.8 46.8 %sum_then_gather.1 = (bf16[8,64,1792]{2,1,0:T(8,128)(2,1)S(1)}, bf16[64,1792]{1,0:T(8,128)(2,1)S(1)}, bf16[4,4,2,56,1536]{4,3,2,1,0:T(8,128)(2,1)S(1)}) custom-call(bf16[8,64,1792]{2,1,0:T(8,128)(2,1)S(1)} %bitcast.10, f32[64,1792]{1,0:T(8,128)S(1)} %copy-done.4, bf16[56,1536]{1,0:T(8,128)(2,1)S(1)} %pad_maximum_fusion.weights), custom_call_target="tpu_custom_call" | custom-call | bytes 100000000 | tf_op jit(solution)/shard_map/sum_then_gather/pallas_call | solution.py:602
  98.5 0.0 copy-start
  98.6 2.4 %copy-done = bf16[4,4,2,56,1536]{4,3,2,1,0:T(8,128)(2,1)} copy-done((bf16[4,4,2,56,1536]{4,3,2,1,0:T(8,128)(2,1)}, bf16[4,4,2,56,1536]{4,3,2,1,0:T(8,128)(2,1)S(1)}, u32[]{:S(2)}) %copy-start) | copy-done | bytes 5505048
  101.0 0.0 copy-done.12
  101.0 6.1 %feed_forward.1 = bf16[512,1792]{1,0:T(8,128)(2,1)S(1)} custom-call(bf16[512,1792]{1,0:T(8,128)(2,1)S(1)} %bitcast.13, f32[1,1792]{1,0:T(1,128)S(1)} %broadcast_in_dim.12.gain, bf16[1792,1536]{1,0:T(8,128)(2,1)} %bitcast.11), custom_call_target="tpu_custom_call" | custom-call | tf_op jit(solution)/shard_map/feed_forward/pallas_call | solution.py:588
  107.0 22.1 %sum_hidden_units.1 = bf16[64,1792]{1,0:T(8,128)(2,1)S(1)} custom-call(bf16[8,64,1792]{2,1,0:T(8,128)(2,1)S(1)} %bitcast.9, bf16[64,1792]{1,0:T(8,128)(2,1)S(1)} %get-tuple-element.16.base), custom_call_target="tpu_custom_call" | custom-call | bytes 50000000 | tf_op jit(solution)/shard_map/sum_hidden_units/pallas_call | solution.py:623
  129.2 0.7 copy.23
  (2 shorter events, 0.0 us)
Async XLA Ops:
  0.0 4.9 %copy-start.2 = (bf16[64,1792]{1,0:T(8,128)(2,1)S(1)}, bf16[64,1792]{1,0:T(8,128)(2,1)}, u32[]{:S(2)}) copy-start(bf16[64,1792]{1,0:T(8,128)(2,1)} %own_hbm.1) | copy-start | bytes 688132
  0.0 4.9 %copy-start.5 = (bf16[2,16,1792]{2,1,0:T(8,128)(2,1)S(1)}, bf16[2,16,1792]{2,1,0:T(8,128)(2,1)}, u32[]{:S(2)}) copy-start(bf16[2,16,1792]{2,1,0:T(8,128)(2,1)} %up_map.1) | copy-start | bytes 344068
  2.1 40.1 %copy-start.6 = (f32[3,2,224]{2,1,0:T(2,128)S(1)}, f32[3,2,224]{2,1,0:T(2,128)}, u32[]{:S(2)}) copy-start(f32[3,2,224]{2,1,0:T(2,128)} %taps.1) | copy-start | bytes 16132
  2.1 40.1 %copy-start.7 = (s32[1,8]{1,0:T(1,128)S(1)}, s32[1,8]{1,0:T(1,128)}, u32[]{:S(2)}) copy-start(s32[1,8]{1,0:T(1,128)} %lengths.1) | copy-start | bytes 100
  2.1 40.1 %copy-start.8 = (s32[8]{0:T(128)S(1)}, s32[8]{0:T(128)}, u32[]{:S(2)}) copy-start(s32[8]{0:T(128)} %param.21) | copy-start | bytes 100
  38.0 1.7 %copy-start.1 = (bf16[4,4,2,56,896]{4,3,2,1,0:T(8,128)(2,1)}, bf16[4,4,2,56,896]{4,3,2,1,0:T(8,128)(2,1)S(1)}, u32[]{:S(2)}) copy-start(bf16[4,4,2,56,896]{4,3,2,1,0:T(8,128)(2,1)S(1)} %get-tuple-element.12) | copy-start | bytes 9633796
  39.7 0.8 copy-start.3
  42.2 9.5 %copy-start.9 = (bf16[512,56]{0,1:T(8,128)(2,1)S(1)}, bf16[512,56]{0,1:T(8,128)(2,1)}, u32[]{:S(2)}) copy-start(bf16[512,56]{0,1:T(8,128)(2,1)} %param.29) | copy-start | bytes 172036
  42.2 9.5 %copy-start.10 = (bf16[56,512]{1,0:T(8,128)(2,1)S(1)}, bf16[56,512]{1,0:T(8,128)(2,1)}, u32[]{:S(2)}) copy-start(bf16[56,512]{1,0:T(8,128)(2,1)} %param.28) | copy-start | bytes 172036
  42.2 9.5 %copy-start.11 = (bf16[56,512]{1,0:T(8,128)(2,1)S(1)}, bf16[56,512]{1,0:T(8,128)(2,1)}, u32[]{:S(2)}) copy-start(bf16[56,512]{1,0:T(8,128)(2,1)} %param.27) | copy-start | bytes 172036
  42.2 9.5 %copy-start.4 = (f32[64,1792]{1,0:T(8,128)S(1)}, f32[64,1792]{1,0:T(8,128)}, u32[]{:S(2)}) copy-start(f32[64,1792]{1,0:T(8,128)} %copy-done.3) | copy-start | bytes 1376260
  51.7 49.2 %copy-start.12 = (f32[1792]{0:T(1024)S(1)}, f32[1792]{0:T(1024)}, u32[]{:S(2)}) copy-start(f32[1792]{0:T(1024)} %param.26) | copy-start | bytes 21508
  98.5 2.4 %copy-start = (bf16[4,4,2,56,1536]{4,3,2,1,0:T(8,128)(2,1)}, bf16[4,4,2,56,1536]{4,3,2,1,0:T(8,128)(2,1)S(1)}, u32[]{:S(2)}) copy-start(bf16[4,4,2,56,1536]{4,3,2,1,0:T(8,128)(2,1)S(1)} %get-tuple-element.15) | copy-start | bytes 16515076
